TPU v7x, 32 devices: a whole 2x2x4 slice. The times are simulated.
32 devices in a mesh: grp: 4 (over y, x), seq: 8 (over z, core).
Axes of the slice: x: 2, y: 2, z: 4, core: 2. Of those that a mesh axis runs over, the one named last changes fastest.
Arguments:
- tokens: bfloat16 [4, 4096, 768], P('grp', 'seq'), may hold values from -6 to 6
- first_values: bfloat16 [4, 4096, 384], P('grp', 'seq'), may hold values from -6 to 6
- placement: int32 [4, 8], P('grp'), may hold values from 0 to 7, each once within a row
- cotangent: bfloat16 [4, 4096, 768], P('grp', 'seq'), may hold values from -6 to 6
- first_norm_gain: bfloat16 [768], P(('grp', 'seq')), may hold values from 0.25 to 1.75
- first_norm_bias: bfloat16 [768], P(('grp', 'seq')), may hold values from -2 to 2
- query_weight: bfloat16 [768, 768], P(('grp', 'seq')), may hold values from -0.25 to 0.25
- query_bias: bfloat16 [768], P(('grp', 'seq')), may hold values from -2 to 2
- key_weight: bfloat16 [768, 768], P(('grp', 'seq')), may hold values from -0.25 to 0.25
- value_weight: bfloat16 [768, 384], P(('grp', 'seq')), may hold values from -0.21875 to 0.21875
- value_bias: bfloat16 [384], P(('grp', 'seq')), may hold values from -2 to 2
- output_weight: bfloat16 [768, 768], P(('grp', 'seq')), may hold values from -1.5 to 1.5
- output_bias: bfloat16 [768], P(('grp', 'seq')), may hold values from -2 to 2
- second_norm_gain: bfloat16 [768], P(('grp', 'seq')), may hold values from 0.25 to 1.75
- second_norm_bias: bfloat16 [768], P(('grp', 'seq')), may hold values from -2 to 2
- expand_weight: bfloat16 [768, 3072], P(('grp', 'seq')), may hold values from -0.21875 to 0.21875
- expand_bias: bfloat16 [3072], P(('grp', 'seq')), may hold values from -2 to 2
- reduce_weight: bfloat16 [3072, 768], P(('grp', 'seq')), may hold values from -0.109375 to 0.109375
- reduce_bias: bfloat16 [768], P(('grp', 'seq')), may hold values from -2 to 2
Outputs:
- layer_output: bfloat16 [4, 4096, 768], P('grp', 'seq')
- token_grad: float32 [4, 4096, 768], P('grp', 'seq')
- first_values_grad: float32 [4, 4096, 384], P('grp', 'seq')
- first_norm_gain_grad: float32 [768], P(('grp', 'seq'))
- first_norm_bias_grad: float32 [768], P(('grp', 'seq'))
- query_weight_grad: float32 [768, 768], P(('grp', 'seq'))
- query_bias_grad: float32 [768], P(('grp', 'seq'))
- key_weight_grad: float32 [768, 768], P(('grp', 'seq'))
- value_weight_grad: float32 [768, 384], P(('grp', 'seq'))
- value_bias_grad: float32 [384], P(('grp', 'seq'))
- output_weight_grad: float32 [768, 768], P(('grp', 'seq'))
- output_bias_grad: float32 [768], P(('grp', 'seq'))
- second_norm_gain_grad: float32 [768], P(('grp', 'seq'))
- second_norm_bias_grad: float32 [768], P(('grp', 'seq'))
- expand_weight_grad: float32 [768, 3072], P(('grp', 'seq'))
- expand_bias_grad: float32 [3072], P(('grp', 'seq'))
- reduce_weight_grad: float32 [3072, 768], P(('grp', 'seq'))
- reduce_bias_grad: float32 [768], P(('grp', 'seq'))
Inputs may be any that keep to these rules, and one draw needn't show every extreme that they name: Each row of placement names every piece of its group once; pieces below 4 are prompt pieces in order, the others continuations.
All inputs are finite; a program needn't handle non-finite values.
Results may differ from a plain program's by a relative error of at most 0.019.
Values may be sent and summed in bfloat16 or wider, within the bound.
A program may use at most 256 MiB of HBM per device.

v0:
```python
import functools
import math

import jax
import jax.numpy as jnp
from jax import lax
from jax.experimental import pallas as pl
from jax.experimental.pallas import tpu as pltpu
from jax.sharding import PartitionSpec as P

MESH = pl.DeviceIdType.MESH


def powers(count):
    out, bit = [], 1
    while bit < count:
        out.append(bit)
        bit *= 2
    return out


def remote(src, dst, send, recv, device):
    return pltpu.make_async_remote_copy(
        src_ref=src, dst_ref=dst, send_sem=send, recv_sem=recv,
        device_id=device, device_id_type=MESH,
    )


def enter(devices):
    barrier = pltpu.get_barrier_semaphore()
    for device in devices:
        pl.semaphore_signal(barrier, inc=1, device_id=device, device_id_type=MESH)
    pl.semaphore_wait(barrier, len(devices))


class Gather:
    def __init__(self, groups, chips, bits, shard, full, chain_send, level_send, recv, pair, own,
                 direct=False):
        self.direct = direct
        self.groups, self.chips, self.bits = groups, chips, bits
        self.shard, self.full = shard, full
        self.chain_send, self.level_send, self.recv, self.pair, self.own = chain_send, level_send, recv, pair, own
        self.g = lax.axis_index("grp")
        seq = lax.axis_index("seq")
        self.s, self.z, self.c = seq, seq // 2, seq % 2

    def block(self, g, z, c):
        return self.full.at[g, z, c]

    def source(self, mask, z, first):
        return self.shard if first else self.block(self.g ^ mask, z, self.c)

    def chain(self, z, step, first):
        side = 0 if step < 0 else 1
        return remote(self.source(0, z, first), self.block(self.g, z, self.c),
                      self.chain_send.at[z, side], self.recv.at[self.g, z],
                      {"seq": self.s + 2 * step})

    def cross(self, level, mask, z, first):
        g = self.g ^ mask
        return remote(self.source(mask, z, first), self.block(g, z, self.c),
                      self.level_send.at[level], self.recv.at[g, z],
                      {"grp": self.g ^ self.bits[level]})

    def held(self, level):
        masks = [0]
        for bit in self.bits[:level]:
            masks = masks + [m ^ bit for m in masks]
        return masks

    def here(self, mask, z):
        g = self.g ^ mask
        pltpu.make_async_copy(self.block(g, z, self.c), self.block(g, z, self.c), self.recv.at[g, z]).wait()

    def begin(self):
        self.begin_chain()
        self.begin_cross()

    def begin_chain(self):
        copy = pltpu.make_async_copy(self.shard, self.block(self.g, self.z, self.c), self.own)
        copy.start()
        if self.direct:
            for out in self.direct_copies():
                out.start()
            return

        @pl.when(self.z > 0)
        def _():
            self.chain(self.z, -1, True).start()

        @pl.when(self.z < self.chips - 1)
        def _():
            self.chain(self.z, 1, True).start()

    def direct_copies(self):
        out = []
        for off in range(1, self.chips):
            chip = lax.rem(self.z + off, self.chips)
            out.append(remote(self.shard, self.block(self.g, self.z, self.c), self.chain_send.at[off, 0],
                              self.recv.at[self.g, self.z], {"seq": 2 * chip + self.c}))
        return out

    def begin_cross(self):
        for level in range(len(self.bits)):
            self.cross(level, 0, self.z, True).start()

    def at(self, distance, body):
        if distance == 0:
            body(self.z, 0)
            return

        @pl.when(self.z >= distance)
        def _():
            body(self.z - distance, 1)

        @pl.when(self.z + distance < self.chips)
        def _():
            body(self.z + distance, -1)

    def along(self, distance):
        self.along_chain(distance)
        self.along_cross(distance)

    def along_chain(self, distance):
        def body(z, step):
            self.here(0, z)
            if self.direct:
                return
            onward = self.z < self.chips - 1 if step > 0 else self.z > 0

            @pl.when(onward)
            def _():
                self.chain(z, step, False).start()

        self.at(distance, body)

    def along_cross(self, distance):
        def body(z, step):
            for level in range(len(self.bits)):
                self.cross(level, 0, z, False).start()

        self.at(distance, body)

    def over(self, level, distance):
        def body(z, step):
            for mask in self.held(level):
                mask = mask ^ self.bits[level]
                self.here(mask, z)
                for later in range(level + 1, len(self.bits)):
                    self.cross(later, mask, z, False).start()

        self.at(distance, body)

    def swap_copy(self):
        mine = self.full.at[:, :, self.c]
        return remote(mine, mine, self.pair.at[0], self.pair.at[1], {"seq": self.s ^ 1})

    def swap(self):
        pltpu.make_async_copy(self.shard, self.shard, self.own).wait()
        self.swap_copy().start()

    def finish(self):
        self.swap_copy().wait_send()
        other = self.full.at[:, :, 1 - self.c]
        pltpu.make_async_copy(other, other, self.pair.at[1]).wait()
        self.sent()

    def sent(self):
        if self.direct:
            for out in self.direct_copies():
                out.wait_send()
        else:
            self.chain_sent()
        for level in range(len(self.bits)):
            sent = self.full.at[pl.ds(0, 2 ** level), :, 0]
            pltpu.make_async_copy(sent, sent, self.level_send.at[level]).wait()

    def chain_sent(self):
        @pl.when(self.z > 0)
        def _():
            self.chain(self.z, -1, True).wait_send()

        @pl.when(self.z < self.chips - 1)
        def _():
            self.chain(self.z, 1, True).wait_send()

        for distance in range(1, self.chips):
            def body(z, step):
                onward = self.z < self.chips - 1 if step > 0 else self.z > 0

                @pl.when(onward)
                def _():
                    self.chain(z, step, False).wait_send()

            self.at(distance, body)


def gather_semaphores(count, groups, chips):
    dma = pltpu.SemaphoreType.DMA
    levels = max(len(powers(groups)), 1)
    return [dma((count, chips, 2)), dma((count, levels)), dma((count, groups, chips)), dma((count, 2)), dma((count,))]


def neighbours(groups, n):
    g, s = lax.axis_index("grp"), lax.axis_index("seq")
    out = [{"grp": g ^ bit} for bit in powers(groups)]
    out += [{"seq": s ^ 1}, {"seq": lax.rem(s + 2, n)}, {"seq": lax.rem(s + n - 2, n)}]
    return out


def gather_kernel(groups, chips, orders, *refs):
    count = len(orders)
    shards, fulls, sems = refs[:count], refs[count:2 * count], refs[2 * count:]
    enter(neighbours(groups, 2 * chips))
    gathers = [Gather(groups, chips, orders[i], shards[i], fulls[i], *[s.at[i] for s in sems]) for i in range(count)]
    run_gathers(gathers)


def run_gathers(gathers):
    chips, levels = gathers[0].chips, len(gathers[0].bits)
    for g in gathers:
        g.begin()
    for distance in range(chips + levels):
        for g in gathers:
            if distance + 1 < chips:
                g.along(distance + 1)
            for level in range(levels):
                if 0 <= distance - level < chips:
                    g.over(level, distance - level)
    for g in gathers:
        g.swap()
    for g in gathers:
        g.finish()


def gather_call(groups, chips, shards, orders):
    count = len(shards)
    return pl.pallas_call(
        functools.partial(gather_kernel, groups, chips, orders),
        out_shape=[jax.ShapeDtypeStruct((groups, chips, 2) + x.shape, x.dtype) for x in shards],
        in_specs=[pl.BlockSpec(memory_space=pl.ANY)] * count,
        out_specs=[pl.BlockSpec(memory_space=pl.ANY)] * count,
        scratch_shapes=gather_semaphores(count, groups, chips),
        compiler_params=pltpu.CompilerParams(collective_id=0, has_side_effects=True),
        name="gather_parameters",
    )(*shards)


class Reduce:
    def __init__(self, groups, chips, bits, partial, shard, own, landed, halves, finals, sems,
                 chain=False, direct=False):
        self.chain, self.direct = chain, direct
        self.groups, self.chips, self.bits = groups, chips, bits
        self.partial, self.shard, self.own, self.landed = partial, shard, own, landed
        self.halves, self.finals, self.mail = halves, finals, halves[0] if direct else None
        self.load, self.pair, self.level_send, self.level_recv, self.chip_send, self.chip_recv = sems
        self.g = lax.axis_index("grp")
        self.s = lax.axis_index("seq")
        self.z, self.c = self.s // 2, self.s % 2

    def masks(self, level):
        out = [0]
        for bit in self.bits[level:]:
            out = out + [m ^ bit for m in out]
        return out

    def load_copy(self):
        return pltpu.make_async_copy(self.partial.at[:, :, self.c], self.own, self.load.at[0])

    def pair_copy(self):
        return remote(self.partial.at[:, :, 1 - self.c], self.landed, self.pair.at[0], self.pair.at[1],
                      {"seq": self.s ^ 1})

    def begin(self):
        self.pair_copy().start()
        self.load_copy().start()

    def paired(self):
        self.load_copy().wait()
        self.pair_copy().wait_recv()

        @pl.loop(0, self.groups)
        def _(g):
            @pl.loop(0, self.chips)
            def _(z):
                self.own[g, z] = self.add(self.own[g, z], self.landed[g, z])

        self.cross_start(0)

    def add(self, a, b):
        return a + b

    def cross_copies(self, level):
        bit = self.bits[level]
        out = []
        for where, mask in enumerate(self.masks(level + 1)):
            out.append(remote(self.own.at[self.g ^ bit ^ mask], self.halves[level].at[where],
                              self.level_send.at[level, where], self.level_recv.at[level, where],
                              {"grp": self.g ^ bit}))
        return out

    def cross_start(self, level):
        if self.direct:
            for copy in self.direct_copies():
                copy.start()
        elif level < len(self.bits):
            for copy in self.cross_copies(level):
                copy.start()
        else:
            self.chip_start()

    def chip_start(self):
        if self.chain:
            self.chain_first()
        else:
            for copy in self.chip_copies():
                copy.start()

    def crossed(self, level, onward=True):
        copies = self.cross_copies(level)
        for where, mask in enumerate(self.masks(level + 1)):
            copies[where].wait_recv()
            g = self.g ^ mask

            @pl.loop(0, self.chips)
            def _(z):
                self.own[g, z] = self.add(self.own[g, z], self.halves[level][where, z])

        if onward:
            self.cross_start(level + 1)

    def chain_copy(self, block, step):
        side = 0 if step > 0 else 1
        return remote(self.own.at[self.g, block], self.finals.at[side, block], self.chip_send.at[side, block],
                      self.chip_recv.at[side, block], {"seq": self.s + 2 * step})

    def chain_add(self, block, side):
        landed = self.finals.at[side, block]
        pltpu.make_async_copy(landed, landed, self.chip_recv.at[side, block]).wait()
        self.own[self.g, block] = self.add(self.own[self.g, block], self.finals[side, block])

    def chain_first(self):
        last = self.chips - 1

        @pl.when(self.z == 0)
        def _():
            for block in range(last, 0, -1):
                self.chain_copy(block, 1).start()

        @pl.when(self.z == last)
        def _():
            for block in range(last):
                self.chain_copy(block, -1).start()

    def chained(self, near_end):
        last = self.chips - 1
        left = self.z < self.chips // 2
        right = jnp.logical_not(left)
        for block in range(last, 0, -1):
            @pl.when((self.z > 0) & (self.z < block) & (left if near_end else right))
            def _():
                self.chain_add(block, 0)
                self.chain_copy(block, 1).start()

        for block in range(last):
            @pl.when((self.z < last) & (self.z > block) & (right if near_end else left))
            def _():
                self.chain_add(block, 1)
                self.chain_copy(block, -1).start()

    def chain_finish(self):
        last = self.chips - 1

        @pl.when(self.z > 0)
        def _():
            self.chain_add(self.z, 0)

        @pl.when(self.z < last)
        def _():
            self.chain_add(self.z, 1)

        self.shard[...] = self.own[self.g, self.z].astype(jnp.float32)

    def chain_drain(self):
        for block in range(self.chips):
            @pl.when(self.z < block)
            def _():
                self.chain_copy(block, 1).wait_send()

            @pl.when(self.z > block)
            def _():
                self.chain_copy(block, -1).wait_send()

    def chip_copies(self):
        out = []
        for off in range(1, self.chips):
            chip = lax.rem(self.z + off, self.chips)
            out.append(remote(self.own.at[self.g, chip], self.finals.at[off - 1], self.chip_send.at[off - 1],
                              self.chip_recv.at[off - 1], {"seq": 2 * chip + self.c}))
        return out

    def direct_copies(self):
        out = []
        for off in range(1, self.groups * self.chips):
            g = lax.rem(self.g + off // self.chips, self.groups)
            z = lax.rem(self.z + off % self.chips, self.chips)
            out.append(remote(self.own.at[g, z], self.mail.at[off // self.chips, off % self.chips],
                              self.level_send.at[off], self.level_recv.at[off], {"grp": g, "seq": 2 * z + self.c}))
        return out

    def direct_finish(self):
        total = self.own[self.g, self.z]
        for off, copy in enumerate(self.direct_copies()):
            copy.wait_recv()
            total = total + self.mail[(off + 1) // self.chips, (off + 1) % self.chips]
        self.shard[...] = total

    def finish(self):
        total = self.own[self.g, self.z].astype(jnp.float32)
        for off, copy in enumerate(self.chip_copies()):
            copy.wait_recv()
            total = total + self.finals[off].astype(jnp.float32)
        self.shard[...] = total

    def drain(self):
        self.pair_copy().wait_send()
        if self.direct:
            for copy in self.direct_copies():
                copy.wait_send()
            return
        for level in range(len(self.bits)):
            for copy in self.cross_copies(level):
                copy.wait_send()
        if self.chain:
            self.chain_drain()
        else:
            for copy in self.chip_copies():
                copy.wait_send()


def reduce_steps(reduces):
    levels = len(reduces[0].bits)
    stages = [lambda r: r.begin(), lambda r: r.paired()]
    for level in range(levels):
        stages.append(lambda r, level=level: r.crossed(level))
    stages += [lambda r: r.finish(), lambda r: r.drain()]
    return [functools.partial(stage, r) for stage in stages for r in reduces]


def direct_scratch(groups, chips, shape):
    vmem, dma = pltpu.VMEM, pltpu.SemaphoreType.DMA
    whole = vmem((groups, chips) + shape[3:5], shape[5])
    count = groups * chips
    return [whole, whole, whole, dma((1,)), dma((2,)), dma((count,)), dma((count,))]


def make_direct(groups, chips, partial, shard, scratch):
    own, landed, mail, load, pair, send, recv = scratch
    return Reduce(groups, chips, powers(groups), partial, shard, own, landed, [mail], None,
                  (load, pair, send, recv, None, None), direct=True)


def reduce_scratch(groups, chips, shapes, chain=False):
    vmem, dma = pltpu.VMEM, pltpu.SemaphoreType.DMA
    levels = len(powers(groups))
    out = []
    for _, _, _, rows, cols, dtype in shapes:
        out += [vmem((groups, chips, rows, cols), dtype), vmem((groups, chips, rows, cols), dtype)]
        out += [vmem((groups >> (level + 1), chips, rows, cols), dtype) for level in range(levels)]
        out += [vmem((2, chips, rows, cols) if chain else (max(chips - 1, 1), rows, cols), dtype)]
        out += [dma((1,)), dma((2,)), dma((max(levels, 1), max(groups // 2, 1))),
                dma((max(levels, 1), max(groups // 2, 1))), dma((2, chips) if chain else (max(chips - 1, 1),)),
                dma((2, chips) if chain else (max(chips - 1, 1),))]
    return out


def make_reduces(groups, chips, orders, partials, shards, scratch, chain=False):
    levels = len(powers(groups))
    each = 2 + levels + 1 + 6
    out = []
    for i, (partial, shard) in enumerate(zip(partials, shards)):
        refs = scratch[i * each : (i + 1) * each]
        out.append(Reduce(groups, chips, orders[i], partial, shard, refs[0], refs[1], refs[2 : 2 + levels],
                          refs[2 + levels], refs[3 + levels :], chain))
    return out


def reduce_kernel(groups, chips, orders, *refs):
    count = len(orders)
    enter(neighbours(groups, 2 * chips))
    for step in reduce_steps(make_reduces(groups, chips, orders, refs[:count], refs[count : 2 * count],
                                          refs[2 * count :])):
        step()


def reduce_call(groups, chips, partials, orders):
    count = len(partials)
    shapes = [p.shape + (p.dtype,) for p in partials]
    return pl.pallas_call(
        functools.partial(reduce_kernel, groups, chips, orders),
        out_shape=[jax.ShapeDtypeStruct(p.shape[3:], jnp.float32) for p in partials],
        in_specs=[pl.BlockSpec(memory_space=pl.ANY)] * count,
        out_specs=[pl.BlockSpec(memory_space=pltpu.VMEM)] * count,
        scratch_shapes=reduce_scratch(groups, chips, shapes),
        compiler_params=pltpu.CompilerParams(collective_id=3, has_side_effects=True, vmem_limit_bytes=64000000),
        name="reduce_gradients",
    )(*partials)


PARTS = 4
NEG = -1e30
EPS = 1e-05


def lanes(shape):
    return lax.broadcasted_iota(jnp.int32, shape, len(shape) - 1)


def swap_lanes(v):
    return pltpu.roll(v, 64, 1)


def fold(v, high):
    half = v.shape[0] // 2
    top, bottom = v[:half], v[half:]
    low = lanes(top.shape) < 64
    if high:
        return jnp.where(low, swap_lanes(top), bottom)
    return jnp.where(low, top, swap_lanes(bottom))


def unfold(v, high):
    low = lanes(v.shape) < 64
    zero = jnp.zeros_like(v)
    if high:
        return jnp.concatenate([jnp.where(low, zero, swap_lanes(v)), jnp.where(low, zero, v)], axis=0)
    return jnp.concatenate([jnp.where(low, v, zero), jnp.where(low, swap_lanes(v), zero)], axis=0)


def product(a, b):
    return lax.dot_general(a, b, (((1,), (0,)), ((), ())), preferred_element_type=jnp.float32)


def product_right(a, b):
    return lax.dot_general(a, b, (((1,), (1,)), ((), ())), preferred_element_type=jnp.float32)


def product_left(a, b):
    return lax.dot_general(a, b, (((0,), (0,)), ((), ())), preferred_element_type=jnp.float32)


def normal_rows(v):
    mean = jnp.mean(v, axis=-1, keepdims=True)
    centred = v - mean
    var = jnp.mean(centred * centred, axis=-1, keepdims=True)
    scale = lax.rsqrt(var + EPS)
    return centred * scale, scale


def pack_heads(v, splits, store):
    size = v.shape[0] // splits
    for tile in range(v.shape[1] // 128):
        for split in range(splits):
            part = v[split * size : (split + 1) * size, tile * 128 : (tile + 1) * 128]
            store(2 * tile, split, fold(part, False))
            store(2 * tile + 1, split, fold(part, True))


def slots_of(table, count):
    out = []
    for piece in range(count):
        slot = jnp.int32(0)
        for place in range(count):
            slot = slot + jnp.where(table[0, place] == piece, place, 0)
        out.append(jnp.minimum(slot, count - 1))
    return out


def pick(values, index):
    out = values[0]
    for i in range(1, len(values)):
        out = jnp.where(index == i, values[i], out)
    return out


class Exchange:
    def __init__(self, n):
        self.n = n
        self.splits = n // PARTS
        self.s = lax.axis_index("seq")
        self.part, self.split = self.s // self.splits, lax.rem(self.s, self.splits)

    def peers(self):
        return [{"seq": lax.rem(self.s + off, self.n)} for off in range(1, self.n)]

    def other(self, off):
        return lax.rem(self.s + off, self.n)

    def scatter(self, j, staged, landed, send, recv):
        out = []
        for off in range(1, self.n):
            t = self.other(off)
            out.append(remote(staged.at[t // self.splits, j, lax.rem(t, self.splits)], landed.at[j, self.s],
                              send.at[j, off - 1], recv.at[j, self.s], {"seq": t}))
        return out

    def own(self, j, staged, landed, recv):
        return pltpu.make_async_copy(staged.at[self.part, j, self.split], landed.at[j, self.s], recv.at[j, self.s])

    def spread(self, j, staged, landed, send, recv):
        out = []
        for off in range(1, PARTS):
            part = lax.rem(self.part + off, PARTS)
            out.append(remote(staged.at[part, j], landed.at[j, self.s], send.at[j, off - 1],
                              recv.at[j, self.s], {"seq": part * self.splits + self.split}))
        return out

    def own_rows(self, j, staged, landed, recv):
        return pltpu.make_async_copy(staged.at[self.part, j], landed.at[j, self.s], recv.at[j, self.s])

    def relay(self, j, off, landed, send, recv):
        slot = lax.rem(self.part + off, PARTS) * self.splits + self.split
        out = []
        for hop in range(1, self.splits):
            split = lax.rem(self.split + hop, self.splits)
            out.append(remote(landed.at[j, slot], landed.at[j, slot], send.at[j, off, hop - 1],
                              recv.at[j, slot], {"seq": self.part * self.splits + split}))
        return slot, out

    def give_back(self, j, heads, staged, landed, send, recv):
        out = []
        row = self.part * heads + j
        for off in range(1, self.n):
            t = self.other(off)
            out.append(remote(staged.at[j, t], landed.at[row, self.split], send.at[j, off - 1],
                              recv.at[j, self.s], {"seq": t}))
        return out

    def keep_own(self, j, heads, staged, landed, recv):
        return pltpu.make_async_copy(staged.at[j, self.s], landed.at[self.part * heads + j, self.split],
                                     recv.at[j, self.s])


def here(ref, sem):
    pltpu.make_async_copy(ref, ref, sem).wait()


def gather_vectors(full, rows, size):
    count = full.shape[0]
    at = lax.broadcasted_iota(jnp.int32, (128, size), 0)
    to = lax.broadcasted_iota(jnp.int32, (128, size), 1)
    place = jnp.where(lax.rem(to, size // count) == at, 1.0, 0.0).astype(jnp.bfloat16)
    some = jnp.concatenate([full[:, row, :].astype(jnp.bfloat16) for row in rows], axis=0)
    spread = product(some, place)
    mine = part_of_lane(count, size)
    return [jnp.sum(jnp.where(mine, spread[i * count : (i + 1) * count], 0.0), axis=0, keepdims=True)
            for i in range(len(rows))]


def forward_kernel(n, groups, heads, orders, sizes, table, x, first, *refs):
    vectors, shards, refs = refs[:9], refs[9:15], refs[15:]
    hidden_out, q_out, kv_out, ol_out, back = refs[:5]
    fulls_out, vectors_out, refs = refs[5:11], refs[11:20], refs[20:]
    hidden_held, q_all, kv_all, ol_all, wq_full, wk_full, wv_full, stores, head_stores = refs[:9]
    fulls, refs = (wq_full, wk_full, wv_full) + fulls_out[3:], refs[9:]
    leaving = [(wq_full, fulls_out[0]), (wk_full, fulls_out[1]), (wv_full, fulls_out[2]), (hidden_held, hidden_out)]

    def leave(i):
        return pltpu.make_async_copy(leaving[i][0], leaving[i][1], stores.at[i])

    def leave_head(j):
        return [pltpu.make_async_copy(held.at[j], out.at[j], head_stores.at[k, j])
                for k, (held, out) in enumerate(((q_all, q_out), (kv_all, kv_out), (ol_all, ol_out)))]

    packed, small_full, q_staged, kv_staged, o_staged, q_work, kv_work = refs[:7]
    q_send, kv_send, relay_send, o_send, q_recv, kv_recv, o_recv = refs[7:14]
    sems = refs[14:]
    ex = Exchange(n)
    chips = n // 2
    bits = powers(groups)
    levels = len(bits)
    enter(ex.peers() + [{"grp": lax.axis_index("grp") ^ bit} for bit in bits])
    gathers = [
        Gather(groups, chips, order, shard, full, *[s.at[i] for s in sems])
        for i, (order, shard, full) in enumerate(zip(orders, (packed,) + shards, (small_full,) + fulls))
    ]
    near, far = gathers[:4], gathers[4:]
    packed[...] = jnp.zeros(packed.shape, jnp.float32)
    for row, vector in enumerate(vectors):
        packed[row : row + 1, : vector.shape[1]] = vector[...].astype(jnp.float32)
    for g in (near[1], near[2], near[3], near[0]):
        g.begin()
    splits = ex.splits
    rows, width = x.shape
    share = rows // splits
    half = n // 2
    fresh = width - first.shape[1]
    normed, _ = normal_rows(x[...].astype(jnp.float32))

    def steps(some, along=1):
        out = []
        for distance in range(chips + levels):
            for g in some:
                if along == 1 and distance + 1 < chips:
                    out.append(functools.partial(g.along, distance + 1))
                if along == 2 and 2 <= distance + 1 < chips:
                    out.append(functools.partial(g.along_cross, distance + 1))
                for level in range(levels):
                    if 0 <= distance - level < chips:
                        out.append(functools.partial(g.over, level, distance - level))
        return out

    order = steps(near)
    cut = (min(len(order), len(near) * (1 + levels)), 3 * len(order) // 4)
    for step in order[: cut[0]]:
        step()
    for g in far:
        g.begin_chain()
    for step in order[cut[0] : cut[1]]:
        step()
    if chips > 1:
        for g in far:
            g.along_chain(1)
    for step in order[cut[1] :]:
        step()
    for g in near:
        g.swap()
    for g in far:
        g.begin_cross()
    for distance in range(1, min(2, chips)):
        for g in far:
            g.along_cross(distance)
    for distance in range(2, chips):
        for g in far:
            g.along_chain(distance)
    for g in near:
        g.finish()
    small = small_full[...].reshape((2 * chips * groups,) + packed.shape)

    def open_vectors(some):
        for size in sorted({sizes[row] for row in some}):
            same = [row for row in some if sizes[row] == size]
            for row, value in zip(same, gather_vectors(small, same, size)):
                vectors_out[row][...] = value

    open_vectors(range(4))
    gain, shift, bq, bv = vectors_out[:4]
    wq, wk, wv = [fulls[i][...].reshape(width, -1) for i in range(3)]
    hidden = (normed * gain[...] + shift[...]).astype(jnp.bfloat16)
    hidden_held[...] = hidden
    for i in range(4):
        leave(i).start()
    for step in range(width // 256):
        cols = slice(step * 256, (step + 1) * 256)
        q = product(hidden, wq[:, cols]) + bq[:, cols]

        def store(head, split, v, step=step):
            head = head + 4 * step
            q_staged[head // heads, head % heads, split] = (v * 0.125).astype(jnp.bfloat16)

        pack_heads(q, splits, store)
        k = product(hidden, wk[:, cols])
        for tile in range(2):
            at = step * 256 + tile * 128
            if at < fresh:
                v = product(hidden, wv[:, at : at + 128]) + bv[:, at : at + 128]
            else:
                v = first[:, at - fresh : at - fresh + 128].astype(jnp.float32)
            kt = k[:, tile * 128 : (tile + 1) * 128]
            low = lanes(kt.shape) < 64
            head = at // 64
            kv_staged[head // heads, head % heads] = jnp.where(low, kt, swap_lanes(v)).astype(jnp.bfloat16)
            head = head + 1
            kv_staged[head // heads, head % heads] = jnp.where(low, swap_lanes(kt), v).astype(jnp.bfloat16)

    @pl.loop(0, heads)
    def _(j):
        for copy in ex.spread(j, kv_staged, kv_all, kv_send, kv_recv):
            copy.start()
        for copy in ex.scatter(j, q_staged, q_all, q_send, q_recv):
            copy.start()
        ex.own(j, q_staged, q_all, q_recv).start()
        ex.own_rows(j, kv_staged, kv_all, kv_recv).start()

    slot = slots_of(table, n)
    row = lax.broadcasted_iota(jnp.int32, (share, rows), 0) + ex.split * share
    own_mask = lax.broadcasted_iota(jnp.int32, (share, rows), 1) <= row

    def piece(j, place, at, keys):
        q = unfold(q_work[at].astype(jnp.float32), False).astype(jnp.bfloat16)
        blocks = [kv_work[k] for k in keys] + [kv_work[at]]
        scores = [product_right(q, block) for block in blocks]
        scores[-1] = jnp.where(own_mask, scores[-1], NEG)
        top = scores[0]
        for s in scores[1:]:
            top = jnp.maximum(top, s)
        top = jnp.max(top, axis=1, keepdims=True)
        total = jnp.zeros((share, rows), jnp.float32)
        out = jnp.zeros((share, 128), jnp.float32)
        for s, block in zip(scores, blocks):
            weight = jnp.exp(s - top)
            total = total + weight
            out = out + product(weight.astype(jnp.bfloat16), block)
        denom = jnp.sum(total, axis=1, keepdims=True)
        out = out / denom
        ol_all[j, place] = jnp.where(lanes(out.shape) < 64, top + jnp.log(denom), out)

    later = steps(far, 2)
    cut = (len(later) // 2, 3 * len(later) // 4)
    for step in later[: cut[0]]:
        step()
    open_vectors(range(4, 9))

    @pl.loop(0, heads)
    def _(j):
        for off in range(PARTS):
            at, copies = ex.relay(j, off, kv_all, relay_send, kv_recv)
            here(kv_all.at[j, at], kv_recv.at[j, at])
            for copy in copies:
                copy.start()
        for t in range(n):
            here(q_all.at[j, t], q_recv.at[j, t])
        for off in range(PARTS):
            for hop in range(1, splits):
                at = lax.rem(ex.part + off, PARTS) * splits + lax.rem(ex.split + hop, splits)
                here(kv_all.at[j, at], kv_recv.at[j, at])
        for t in range(n):
            q_work[t] = q_all[j, t]
            kv_work[t] = kv_all[j, t]

        @pl.loop(0, half)
        def _(c):
            piece(j, half + c, pick(slot[half:], c), slot[:half])

        for p in range(half):
            piece(j, p, slot[p], slot[:p])
        for t in range(n):
            o_staged[j, t] = fold(ol_all[j, table[0, t]], True).astype(jnp.bfloat16)
        for copy in ex.give_back(j, heads, o_staged, back, o_send, o_recv):
            copy.start()
        ex.keep_own(j, heads, o_staged, back, o_recv).start()
        for copy in leave_head(j):
            copy.start()

        @pl.when(j == 0)
        def _():
            for step in later[cut[0] : cut[1]]:
                step()

        @pl.when(j == min(1, heads - 1))
        def _():
            for step in later[cut[1] :]:
                step()
            for g in far:
                g.swap()

    @pl.loop(0, heads)
    def _(j):
        for copy in ex.spread(j, kv_staged, kv_all, kv_send, kv_recv):
            copy.wait_send()
        for copy in ex.scatter(j, q_staged, q_all, q_send, q_recv):
            copy.wait_send()
        for off in range(PARTS):
            for copy in ex.relay(j, off, kv_all, relay_send, kv_recv)[1]:
                copy.wait_send()
        for copy in ex.give_back(j, heads, o_staged, back, o_send, o_recv):
            copy.wait_send()
        for t in range(n):
            landed = back.at[t // splits * heads + j, t % splits]
            here(landed, o_recv.at[j, t])
    for g in far:
        g.finish()
    for i in range(4):
        leave(i).wait()

    @pl.loop(0, heads)
    def _(j):
        for copy in leave_head(j):
            copy.wait()


def forward_call(n, groups, table, x, first, vectors, shards):
    rows, width = x.shape
    splits = n // PARTS
    chips = n // 2
    heads = width // 64 // PARTS
    share = rows // splits
    low = jnp.bfloat16
    vmem, dma = pltpu.VMEM, pltpu.SemaphoreType.DMA
    inside, outside = pl.BlockSpec(memory_space=vmem), pl.BlockSpec(memory_space=pl.ANY)
    shape = jax.ShapeDtypeStruct
    bits = powers(groups)
    forth, behind = bits, bits[::-1]
    sizes = [v.shape[1] * groups * n for v in vectors]
    block = (groups, chips, 2)
    return pl.pallas_call(
        functools.partial(forward_kernel, n, groups, heads, [forth, forth, behind, forth, behind, forth, behind], sizes),
        out_shape=[
            shape((rows, width), low),
            shape((heads, n, share // 2, 128), low),
            shape((heads, n, rows, 128), low),
            shape((heads, n, share, 128), jnp.float32),
            shape((PARTS * heads, splits, share // 2, 128), low),
        ]
        + [shape(block + w.shape, low) for w in shards]
        + [shape((1, size), jnp.float32) for size in sizes],
        in_specs=[pl.BlockSpec(memory_space=pltpu.SMEM)] + [inside] * 11 + [outside] * 6,
        out_specs=[outside] * 4 + [inside] + [outside] * 6 + [inside] * 9,
        scratch_shapes=[
            vmem((rows, width), low),
            vmem((heads, n, share // 2, 128), low),
            vmem((heads, n, rows, 128), low),
            vmem((heads, n, share, 128), jnp.float32),
        ]
        + [vmem(block + w.shape, low) for w in shards[:3]]
        + [
            dma((4,)),
            dma((3, heads)),
            vmem((16, 128), jnp.float32),
            vmem(block + (16, 128), jnp.float32),
            vmem((PARTS, heads, splits, share // 2, 128), low),
            vmem((PARTS, heads, rows, 128), low),
            vmem((heads, n, share // 2, 128), low),
            vmem((n, share // 2, 128), low),
            vmem((n, rows, 128), low),
            dma((heads, n - 1)),
            dma((heads, PARTS - 1)),
            dma((heads, PARTS, max(splits - 1, 1))),
            dma((heads, n - 1)),
            dma((heads, n)),
            dma((heads, n)),
            dma((heads, n)),
        ]
        + gather_semaphores(7, groups, chips),
        compiler_params=pltpu.CompilerParams(
            collective_id=1, has_side_effects=True, vmem_limit_bytes=64000000
        ),
        name="attention_forward",
    )(table, x, first, *vectors, *shards)


def join_tiles(even, odd, high):
    low = lanes(even.shape) < 64
    if high:
        return jnp.where(low, swap_lanes(even), odd)
    return jnp.where(low, even, swap_lanes(odd))


def join_rows(back):
    heads, splits = back.shape[0], back.shape[1]
    tiles = []
    for tile in range(heads // 2):
        parts = []
        for split in range(splits):
            even = back[2 * tile, split].astype(jnp.float32)
            odd = back[2 * tile + 1, split].astype(jnp.float32)
            parts += [join_tiles(even, odd, False), join_tiles(even, odd, True)]
        tiles.append(jnp.concatenate(parts, axis=0))
    return jnp.concatenate(tiles, axis=1)


def own_columns(j, heads, wq, wk, wv):
    def column(w, head):
        tile = w[:, head // 2 * 128 : head // 2 * 128 + 128].astype(jnp.float32)
        return tile, head % 2

    tiles = []
    for w in (wq, wk, wv):
        for part in range(0, w.shape[1] // 64 // heads, 2):
            (a, high_a), (b, high_b) = column(w, part * heads + j), column(w, (part + 1) * heads + j)
            a = swap_lanes(a) if high_a else a
            b = b if high_b else swap_lanes(b)
            tiles.append(jnp.where(lanes(a.shape) < 64, a, b).astype(jnp.bfloat16))
    return jnp.concatenate(tiles, axis=1)


def in_order(some, at, parts):
    heads = len(some)
    tiles = []
    for head in range(0, heads * parts, 2):
        def column(h):
            j, part = h % heads, h // heads
            start = at + part // 2 * 128
            return some[j][:, start : start + 128], part % 2

        (a, high_a), (b, high_b) = column(head), column(head + 1)
        a = swap_lanes(a) if high_a else a
        b = b if high_b else swap_lanes(b)
        tiles.append(jnp.where(lanes(a.shape) < 64, a, b))
    return jnp.concatenate(tiles, axis=1)


def own_vectors(sums, parts, fresh_parts):
    sums = [jnp.broadcast_to(s, (8, s.shape[1])) for s in sums]
    return [in_order(sums, 0, parts)[0:1], in_order(sums, parts * 128, fresh_parts)[0:1]]


def part_of_lane(count, size):
    part = size // count
    lane = lax.broadcasted_iota(jnp.int32, (count, size), 1)
    row = lax.broadcasted_iota(jnp.int32, (count, size), 0)
    return (lane >= row * part) & (lane < row * part + part)


def spread_vectors(vectors, count):
    size = vectors[0].shape[1]
    mine = part_of_lane(count, size)
    at = lax.broadcasted_iota(jnp.int32, (size, 128), 0)
    to = lax.broadcasted_iota(jnp.int32, (size, 128), 1)
    pick_part = jnp.where(lax.rem(at, size // count) == to, 1.0, 0.0).astype(jnp.bfloat16)
    rows = []
    for vector in vectors:
        value = jnp.where(mine, vector, 0.0)
        for _ in range(3):
            high = value.astype(jnp.bfloat16)
            rows.append(high)
            value = value - high.astype(jnp.float32)
    out = product(jnp.concatenate(rows, axis=0), pick_part)
    parts = [out[i * count : (i + 1) * count] for i in range(len(rows))]
    return [(parts[3 * i] + parts[3 * i + 1] + parts[3 * i + 2]).reshape(count, 1, 128) for i in range(len(vectors))]


def backward_kernel(
    n, groups, heads, orders_far, orders_near,
    table, do_in, gain, s_gain2, s_bias2, s_ob, s_eb, s_rb, q_in, kv_in, ol_in, hidden_in, x_in, dmid_in,
    wq_in, wk_in, wv_in, *refs,
):
    count = len(orders_far)
    far_in, refs = refs[:count], refs[count:]
    token_grad, first_grad = refs[:2]
    far_out, refs = refs[2 : 2 + count], refs[2 + count :]
    near_out, refs = refs[: 2 * heads + 1], refs[2 * heads + 1 :]
    do_all, do_work, acc, dq_piece, dq_staged, part_staged, part_all, dkv_staged, dq_back, dkv_back = refs[:10]
    refs = refs[10:]
    near_in, refs = refs[: 2 * heads + 1], refs[2 * heads + 1 :]
    weights, h_across, refs = refs[:heads], refs[heads], refs[heads + 1 :]
    q_all, kv_all, ol_all, hidden, x, dmid, wq, wk, wv, loads = refs[:10]
    refs = refs[10:]
    do_send, do_recv, dq_send, dq_recv, part_send, part_recv, dkv_send, dkv_recv = refs[:8]
    scratch = refs[8:]

    def full_copy(source, held, at):
        pltpu.make_async_copy(source, held, loads.at[at]).wait()
        return held

    entering = [(hidden_in, hidden, 3), (wq_in, wq, 6), (wk_in, wk, 7), (wv_in, wv, 8), (q_in, q_all, 0),
                (kv_in, kv_all, 1), (ol_in, ol_all, 2), (x_in, x, 4), (dmid_in, dmid, 5)]
    ex = Exchange(n)
    chips = n // 2
    g, z, c = lax.axis_index("grp"), ex.s // 2, lax.rem(ex.s, 2)
    enter(ex.peers() + [
        {"grp": lax.rem(g + off // chips, groups), "seq": 2 * lax.rem(z + off % chips, chips) + c}
        for off in range(chips, groups * chips)
    ])
    small = make_direct(groups, chips, near_in[-1], near_out[-1], scratch[-7:])
    scratch = scratch[:-7]
    each = len(scratch) // (count + 2 * heads)
    far = make_reduces(groups, chips, orders_far, far_in, far_out, scratch[: count * each], True)
    near = make_reduces(groups, chips, orders_near, near_in[:-1], near_out[:-1], scratch[count * each :])
    near_last = near[-2:]
    near_first = near[:-2]
    splits = ex.splits
    rows = kv_all.shape[2]
    share = rows // splits
    half = n // 2
    fresh = wv.shape[1]

    @pl.loop(0, heads)
    def _(j):
        for copy in ex.scatter(j, do_in, do_all, do_send, do_recv):
            copy.start()
        ex.own(j, do_in, do_all, do_recv).start()

    for source, held, at in entering:
        pltpu.make_async_copy(source, held, loads.at[at]).start()
    for r in far:
        r.begin()
    for source, held, at in entering[:7]:
        full_copy(source, held, at)
    low = jnp.bfloat16
    fresh_parts = PARTS * fresh // x.shape[1]
    h_across[...] = jnp.transpose(hidden[...])
    for j in range(heads):
        weights[j][...] = own_columns(j, heads, wq, wk, wv)
    slot = slots_of(table, n)
    column = lax.broadcasted_iota(jnp.int32, (rows, share), 1) + ex.split * share
    own_mask = lax.broadcasted_iota(jnp.int32, (rows, share), 0) <= column

    def piece(j, place, at, keys):
        q = unfold(q_all[j, at].astype(jnp.float32), False).astype(jnp.bfloat16)
        grad = unfold(do_work[at].astype(jnp.float32), True)
        ol = ol_all[j, place]
        delta = jnp.sum(jnp.transpose(grad * ol), axis=0, keepdims=True)
        logsum = jnp.transpose(ol)[0:1]
        grad = grad.astype(jnp.bfloat16)

        def block_terms(key_place, key_slot, mask):
            block = kv_all[j, key_slot]
            weight = jnp.exp(product_right(block, q) - logsum)
            if mask:
                weight = jnp.where(own_mask, weight, 0.0)
            change = (weight * (product_right(block, grad) - delta)).astype(jnp.bfloat16)
            term = product(weight.astype(jnp.bfloat16), grad) + product(change, q)
            acc[key_place] = acc[key_place] + term
            return product_left(block, change)

        dq = block_terms(place, at, True)
        if len(keys) in (2, 3):
            slots = [s for _, s in keys]
            dq = lax.fori_loop(0, len(keys), lambda k, v: v + block_terms(k, pick(slots, k), False), dq)
        else:
            for key_place, key_slot in keys:
                dq = dq + block_terms(key_place, key_slot, False)
        dq_piece[place] = fold(jnp.transpose(dq) * 0.125, False).astype(jnp.bfloat16)

    def part_copies(j):
        out = []
        for hop in range(1, splits):
            split = lax.rem(ex.split + hop, splits)
            for part in range(PARTS):
                out.append(remote(part_staged.at[j, hop - 1, part], part_all.at[j, hop - 1, part],
                                  part_send.at[j, hop - 1, part], part_recv.at[j, hop - 1, part],
                                  {"seq": ex.part * splits + split}))
        return out

    def back_copies(j):
        out = []
        row = ex.part * heads + j
        for off in range(1, PARTS):
            part = lax.rem(ex.part + off, PARTS)
            out.append(remote(dkv_staged.at[j, part], dkv_back.at[row], dkv_send.at[j, off - 1],
                              dkv_recv.at[j, ex.part], {"seq": part * splits + ex.split}))
        return out

    @pl.loop(0, heads)
    def _(j):
        for t in range(n):
            here(do_all.at[j, t], do_recv.at[j, t])
        for t in range(n):
            do_work[t] = do_all[j, t]
            acc[t] = jnp.zeros((rows, 128), jnp.float32)

        @pl.loop(0, half)
        def _(c):
            piece(j, half + c, pick(slot[half:], c), [(p, slot[p]) for p in range(half)])

            @pl.when((j == 0) & (c == 1))
            def _():
                for r in far:
                    r.paired()

            @pl.when((j == heads - 1) & (c == 1))
            def _():
                for r in far:
                    r.crossed(0)

        for p in range(half):
            piece(j, p, slot[p], [(k, slot[k]) for k in range(p)])
        for hop in range(1, splits):
            split = lax.rem(ex.split + hop, splits)
            for part in range(PARTS):
                part_staged[j, hop - 1, part] = acc[table[0, part * splits + split]].astype(jnp.bfloat16)
        for copy in part_copies(j):
            copy.start()
        for t in range(n):
            dq_staged[j, t] = dq_piece[table[0, t]]
        for hop in range(1, splits):
            for part in range(PARTS):
                here(part_all.at[j, hop - 1, part], part_recv.at[j, hop - 1, part])
        for part in range(PARTS):
            total = acc[table[0, part * splits + ex.split]]
            for hop in range(1, splits):
                total = total + part_all[j, hop - 1, part].astype(jnp.float32)
            dkv_staged[j, part] = total.astype(jnp.bfloat16)
        for copy in back_copies(j):
            copy.start()
        pltpu.make_async_copy(dkv_staged.at[j, ex.part], dkv_back.at[ex.part * heads + j],
                              dkv_recv.at[j, ex.part]).start()
        for copy in ex.give_back(j, heads, dq_staged, dq_back, dq_send, dq_recv):
            copy.start()
        ex.keep_own(j, heads, dq_staged, dq_back, dq_recv).start()

    levels = len(powers(groups))

    def total(v):
        return jnp.sum(v, axis=0, keepdims=True)

    def project(j):
        for t in range(n):
            here(dq_back.at[t // splits * heads + j, t % splits], dq_recv.at[j, t])
        for part in range(PARTS):
            here(dkv_back.at[part * heads + j], dkv_recv.at[j, part])
        tiles = []
        for part in range(0, PARTS, 2):
            a, b = part * heads + j, part * heads + heads + j
            parts = []
            for split in range(splits):
                even, odd = dq_back[a, split].astype(jnp.float32), dq_back[b, split].astype(jnp.float32)
                parts += [join_tiles(even, odd, False), join_tiles(even, odd, True)]
            tiles.append(jnp.concatenate(parts, axis=0))
        pairs = [(dkv_back[part * heads + j].astype(jnp.float32), dkv_back[(part + 1) * heads + j].astype(jnp.float32))
                 for part in range(0, PARTS, 2)]
        tiles += [join_tiles(a, b, False) for a, b in pairs]
        tiles += [join_tiles(a, b, True) for a, b in pairs[: fresh_parts // 2]]
        grad = jnp.concatenate(tiles, axis=1)
        sums = total(grad)
        grad = grad.astype(low)
        for ref, r, value in ((near_in[2 * j + 1], near[2 * j + 1], grad[:, PARTS * 64 :]),
                              (near_in[2 * j], near[2 * j], grad[:, : PARTS * 64])):
            ref[...] = product(h_across[...], value).reshape(ref.shape).astype(low)
            r.begin()
        return product_right(grad, weights[j][...]), sums

    devices = groups * n
    ob, gain2, bias2, rb = spread_vectors([s_ob[...], s_gain2[...], s_bias2[...], s_rb[...]], devices)
    later_rows = [ob, gain2, bias2] + spread_vectors([s_eb[...]], devices) + [rb]
    later_rows.append(jnp.zeros((devices, 16 - 9, 128), jnp.float32))
    done = [project(0)]
    for r in far:
        for level in range(1, levels):
            r.crossed(level)
    done += [project(j) for j in range(1, heads - 1)]
    for r in near_first:
        r.paired()
    normed, scale = normal_rows(full_copy(x_in, x, 4)[...].astype(jnp.float32))
    for level in range(levels - 1):
        for r in near_first:
            r.crossed(level)
    done.append(project(heads - 1))
    for r in far:
        r.chained(True)
    for r in near_first:
        r.crossed(levels - 1)
    dh = done[0][0]
    for more, _ in done[1:]:
        dh = dh + more
    for r in near_last:
        r.paired()
    sums = [total(dh * normed), total(dh)]
    sum_q, sum_v = own_vectors([s for _, s in done], PARTS, fresh_parts)
    first_rows = spread_vectors(sums + [sum_q], devices) + spread_vectors([sum_v], devices)
    spread = jnp.concatenate(first_rows + later_rows, axis=1)
    near_in[-1][...] = spread.reshape(near_in[-1].shape)
    small.begin()
    for level in range(levels):
        for r in near_last:
            r.crossed(level)
        if level == 0:
            small.paired()
    scaled = dh * gain[...].astype(jnp.float32)
    inner = jnp.mean(scaled, axis=-1, keepdims=True)
    along = jnp.mean(scaled * normed, axis=-1, keepdims=True)
    token_grad[...] = full_copy(dmid_in, dmid, 5)[...] + scale * (scaled - inner - normed * along)
    for pair in range(fresh // 64, PARTS * heads, 2):
        even, odd = dkv_back[pair].astype(jnp.float32), dkv_back[pair + 1].astype(jnp.float32)
        first_grad[:, pair * 64 - fresh : pair * 64 - fresh + 128] = join_tiles(even, odd, True)
    for r in far:
        r.chained(False)
    for r in far:
        r.chain_finish()
    for r in near:
        r.finish()
    small.direct_finish()
    for r in far + near + [small]:
        r.drain()

    @pl.loop(0, heads)
    def _(j):
        for copy in ex.scatter(j, do_in, do_all, do_send, do_recv):
            copy.wait_send()
        for copy in part_copies(j):
            copy.wait_send()
        for copy in back_copies(j):
            copy.wait_send()
        for copy in ex.give_back(j, heads, dq_staged, dq_back, dq_send, dq_recv):
            copy.wait_send()


def backward_call(n, groups, table, do_in, q_all, kv_all, ol_all, hidden, x, gain, wq, wk, wv, dmid, sums, far):
    heads, _, rows, _ = kv_all.shape
    splits = n // PARTS
    chips = n // 2
    share = rows // splits
    width, fresh = wv.shape
    low = jnp.bfloat16
    vmem, dma = pltpu.VMEM, pltpu.SemaphoreType.DMA
    inside = pl.BlockSpec(memory_space=vmem)
    shape = jax.ShapeDtypeStruct
    bits = powers(groups)
    forth, back = bits, bits[::-1]
    block = (groups, chips, 2)
    part = width // (groups * n)
    wide = 2 * PARTS * 64 + PARTS * 64 * fresh // width
    near = [block + (part, PARTS * 64, low), block + (part, wide - PARTS * 64, low)] * heads
    near += [block + (16, 128, jnp.float32)]
    shapes = [f.shape + (low,) for f in far] + near
    return pl.pallas_call(
        functools.partial(backward_kernel, n, groups, heads, [forth, back, forth][: len(far)],
                          [(forth, back)[j % 2] for j in range(2 * heads)]),
        out_shape=[shape((rows, width), jnp.float32), shape((rows, width - fresh), jnp.float32)]
        + [shape(s[3:5], jnp.float32) for s in shapes],
        in_specs=[pl.BlockSpec(memory_space=pltpu.SMEM)] + [inside] * 7
        + [pl.BlockSpec(memory_space=pl.ANY)] * (9 + len(far)),
        out_specs=[inside] * (3 + 2 * heads + len(far)),
        scratch_shapes=[
            vmem((heads, n, share // 2, 128), low),
            vmem((n, share // 2, 128), low),
            vmem((n, rows, 128), jnp.float32),
            vmem((n, share // 2, 128), low),
            vmem((heads, n, share // 2, 128), low),
            vmem((heads, max(splits - 1, 1), PARTS, rows, 128), low),
            vmem((heads, max(splits - 1, 1), PARTS, rows, 128), low),
            vmem((heads, PARTS, rows, 128), low),
            vmem((PARTS * heads, splits, share // 2, 128), low),
            vmem((PARTS * heads, rows, 128), low),
        ]
        + [vmem(s[:5], s[5]) for s in near]
        + [vmem((width, wide), low)] * heads
        + [vmem((width, rows), low)]
        + [vmem(v.shape, v.dtype) for v in (q_all, kv_all, ol_all, hidden, x, dmid, wq, wk, wv)]
        + [
            dma((9,)),
            dma((heads, n - 1)),
            dma((heads, n)),
            dma((heads, n - 1)),
            dma((heads, n)),
            dma((heads, max(splits - 1, 1), PARTS)),
            dma((heads, max(splits - 1, 1), PARTS)),
            dma((heads, PARTS - 1)),
            dma((heads, PARTS)),
        ]
        + reduce_scratch(groups, chips, shapes[: len(far)], True)
        + reduce_scratch(groups, chips, shapes[len(far) : -1])
        + direct_scratch(groups, chips, shapes[-1]),
        compiler_params=pltpu.CompilerParams(
            collective_id=2, has_side_effects=True, vmem_limit_bytes=67043328
        ),
        name="attention_backward",
    )(table, do_in, gain, *sums, q_all, kv_all, ol_all, hidden, x, dmid, wq, wk, wv, *far)


def hand_over_kernel(count, heads, sizes, fresh_parts, *refs):
    ins, refs = refs[:count], refs[count:]
    near, small, refs = refs[: 2 * heads], refs[2 * heads], refs[2 * heads + 1 :]
    outs, refs = refs[:count], refs[count:]
    g_wq, g_wk, g_wv = refs[:3]
    vectors, refs = refs[3 : 3 + len(sizes)], refs[3 + len(sizes) :]
    held, loads, stores = refs[:-2], refs[-2], refs[-1]
    for i in range(count):
        pltpu.make_async_copy(ins[i], held[i], loads.at[i]).start()
    some = [ref[...] for ref in near]
    g_wq[...] = in_order(some[::2], 0, PARTS)
    g_wk[...] = in_order(some[1::2], 0, PARTS)
    g_wv[...] = in_order(some[1::2], PARTS * 64, fresh_parts)
    for row, size in enumerate(sizes):
        vectors[row][...] = small[row : row + 1, :size]
    for i in range(count):
        pltpu.make_async_copy(ins[i], held[i], loads.at[i]).wait()
        pltpu.make_async_copy(held[i], outs[i], stores.at[i]).start()
    for i in range(count):
        pltpu.make_async_copy(held[i], outs[i], stores.at[i]).wait()


def hand_over(arrays, near, small, sizes, width, fresh):
    shape = jax.ShapeDtypeStruct
    count, heads = len(arrays), len(near) // 2
    rows = near[0].shape[0]
    inside, outside = pl.BlockSpec(memory_space=pltpu.VMEM), pl.BlockSpec(memory_space=pl.ANY)
    return pl.pallas_call(
        functools.partial(hand_over_kernel, count, heads, sizes, PARTS * fresh // width),
        out_shape=[shape(a.shape, a.dtype) for a in arrays]
        + [shape((rows, size), jnp.float32) for size in (width, width, fresh)]
        + [shape((1, size), jnp.float32) for size in sizes],
        in_specs=[outside] * count + [inside] * (2 * heads + 1),
        out_specs=[outside] * count + [inside] * (3 + len(sizes)),
        scratch_shapes=[pltpu.VMEM(a.shape, a.dtype) for a in arrays]
        + [pltpu.SemaphoreType.DMA((count,)), pltpu.SemaphoreType.DMA((count,))],
        compiler_params=pltpu.CompilerParams(vmem_limit_bytes=60000000),
        name="hand_over",
    )(*arrays, *near, small)


def feed_kernel(
    parts, heads, back, x, dy, bo, gain, shift, be, br, wo_in, we_in, wr_in,
    out, dmid_out, do_staged, s_gain, s_shift, s_ob, s_eb, s_rb, g_we, g_wr, g_wo,
    wo, we, wr, k_we, k_wr, k_wo, dh, load, keep,
):
    low = jnp.bfloat16
    rows, width = x.shape
    step = we.shape[1] // parts
    splits = back.shape[1]

    def total(v):
        return jnp.sum(v, axis=0, keepdims=True)

    def columns(c):
        return pl.ds(pl.multiple_of(c * step, 128), step)

    def fetch(c):
        return (pltpu.make_async_copy(we_in.at[:, columns(c)], we.at[:, columns(c)], load.at[c]),
                pltpu.make_async_copy(wr_in.at[columns(c)], wr.at[columns(c)], load.at[parts + c]))

    def store(c):
        return (pltpu.make_async_copy(k_we.at[:, columns(c)], g_we.at[:, columns(c)], keep.at[c]),
                pltpu.make_async_copy(k_wr.at[columns(c)], g_wr.at[columns(c)], keep.at[parts + c]))

    first = pltpu.make_async_copy(wo_in, wo, load.at[2 * parts])
    first.start()
    for c in range(parts):
        for copy in fetch(c):
            copy.start()
    att = join_rows(back).astype(low)
    first.wait()
    mid = x[...].astype(jnp.float32) + product(att, wo[...]) + bo[...]
    normed, scale = normal_rows(mid)
    second = (normed * gain[...] + shift[...]).astype(low)
    second_across = jnp.transpose(second)
    seed = dy[...]
    seed_full = seed.astype(jnp.float32)
    s_rb[...] = total(seed_full)
    dmid_out[...] = mid + br[...]
    dh[...] = jnp.zeros((rows, width), jnp.float32)

    @pl.loop(0, parts)
    def _(c):
        for copy in fetch(c):
            copy.wait()
        expand, reduce = we[:, columns(c)], wr[columns(c)]
        u = product(second, expand) + be[:, columns(c)]
        square = u * u
        t = jnp.tanh(math.sqrt(2 / math.pi) * (u + 0.044715 * (u * square)))
        z = (0.5 * u * (1.0 + t)).astype(low)
        slope = 0.5 * (1.0 + t) + (0.5 * math.sqrt(2 / math.pi)) * u * (1.0 - t * t) * (1.0 + (3 * 0.044715) * square)
        du_full = (slope * product_right(seed, reduce)).astype(low)
        s_eb[:, columns(c)] = total(du_full.astype(jnp.float32))
        dmid_out[...] += product(z, reduce)
        dh[...] += product_right(du_full, expand)
        k_wr[columns(c)] = product(jnp.transpose(z), seed).astype(low)
        k_we[:, columns(c)] = product(second_across, du_full).astype(low)
        for copy in store(c):
            copy.start()

    out[...] = dmid_out[...].astype(low)
    back_normed = dh[...]
    s_gain[...] = total(back_normed * normed)
    s_shift[...] = total(back_normed)
    scaled = back_normed * gain[...]
    inner = jnp.mean(scaled, axis=-1, keepdims=True)
    along = jnp.mean(scaled * normed, axis=-1, keepdims=True)
    dmid = seed_full + scale * (scaled - inner - normed * along)
    dmid_out[...] = dmid
    branch = dmid.astype(low)
    s_ob[...] = total(branch.astype(jnp.float32))
    k_wo[...] = product(jnp.transpose(att), branch).astype(low)
    last = pltpu.make_async_copy(k_wo, g_wo, keep.at[2 * parts])
    last.start()
    for group in range(width // 256):
        datt = product_right(branch, wo[group * 256 : (group + 1) * 256, :])

        def put(head, split, v, group=group):
            head = head + 4 * group
            do_staged[head // heads, head % heads, split] = v.astype(low)

        pack_heads(datt, splits, put)
    for c in range(parts):
        for copy in store(c):
            copy.wait()
    last.wait()


def feed_call(back, x, dy, bo, gain, shift, be, br, wo, we, wr):
    rows, width = x.shape
    inner = we.shape[1]
    parts = inner // width
    heads = back.shape[0] // PARTS
    splits = back.shape[1]
    low, full = jnp.bfloat16, jnp.float32
    vmem, dma = pltpu.VMEM, pltpu.SemaphoreType.DMA
    inside, outside = pl.BlockSpec(memory_space=vmem), pl.BlockSpec(memory_space=pl.ANY)
    shape = jax.ShapeDtypeStruct
    return pl.pallas_call(
        functools.partial(feed_kernel, parts, heads),
        out_shape=[
            shape((rows, width), low),
            shape((rows, width), full),
            shape((PARTS, heads) + back.shape[1:], low),
            shape((1, width), full),
            shape((1, width), full),
            shape((1, width), full),
            shape((1, inner), full),
            shape((1, width), full),
            shape(we.shape, low),
            shape(wr.shape, low),
            shape(wo.shape, low),
        ],
        in_specs=[inside] * 8 + [outside] * 3,
        out_specs=[inside] * 8 + [outside] * 3,
        scratch_shapes=[
            vmem(wo.shape, low), vmem(we.shape, low), vmem(wr.shape, low),
            vmem(we.shape, low), vmem(wr.shape, low), vmem(wo.shape, low),
            vmem((rows, width), full),
            dma((2 * parts + 1,)), dma((2 * parts + 1,)),
        ],
        compiler_params=pltpu.CompilerParams(vmem_limit_bytes=64000000),
        name="feed_forward",
    )(back, x, dy, bo, gain, shift, be, br, wo, we, wr)


def body(
    tokens,
    first_values,
    placement,
    cotangent,
    *parts,
):
    groups, rows, width = tokens.shape
    n = lax.axis_size("seq")
    small = (0, 1, 3, 6, 8, 9, 10, 12, 14)
    large = (2, 4, 5, 7, 11, 13)
    done = forward_call(n, lax.axis_size("grp"), placement, tokens[0], first_values[0],
                        [parts[i][None] for i in small], [parts[i] for i in large])
    hidden, q_all, kv_all, ol_all, back = done[:5]
    whole = [None] * 15
    for i, v in zip(large, done[5:11]):
        whole[i] = v.reshape(-1, v.shape[-1])
    for i, v in zip(small, done[11:]):
        whole[i] = v[0]
    layer_output, dmid, do_staged, *sums, g_we, g_wr, g_wo = feed_call(
        back, tokens[0], cotangent[0], whole[8][None], whole[9][None], whole[10][None], whole[12][None],
        whole[14][None], whole[7], whole[11], whole[13],
    )
    block = (lax.axis_size("grp"), n // 2, 2)
    far = [v.reshape(block + (-1, v.shape[1])) for v in (g_we, g_wr, g_wo)]
    inside = far if n <= 8 else []
    done = backward_call(
        n, block[0], placement, do_staged, q_all, kv_all, ol_all, hidden, tokens[0],
        whole[0][None], whole[2], whole[4], whole[5], dmid, [sums[0], sums[1], sums[2], sums[3], sums[4]],
        inside,
    )
    token_grad, first_grad = done[:2]
    if not inside:
        forth = powers(block[0])
        done = done[:2] + reduce_call(block[0], block[1], far, [forth, forth[::-1], forth]) + done[2:]
    g_we, g_wr, g_wo = done[2:5]
    near, g_small = done[5:-1], done[-1]
    sizes = [parts[i].shape[0] for i in small]
    out = hand_over([token_grad, first_grad, g_wo, g_we, g_wr], near, g_small, sizes, whole[2].shape[1], whole[5].shape[1])
    owned = [None] * 15
    for i, v in zip((7, 11, 13, 2, 4, 5), out[2:8]):
        owned[i] = v
    for i, v in zip(small, out[8:]):
        owned[i] = v.reshape(-1)
    return (layer_output[None], out[0][None], out[1][None]) + tuple(owned)


def solution(mesh):
    spread = P("grp", "seq", None)
    both = ("grp", "seq")
    vector, matrix = P(both), P(both, None)
    kinds = (vector, vector, matrix, vector, matrix, matrix, vector, matrix, vector, vector, vector,
             matrix, vector, matrix, vector)
    in_specs = (spread, spread, P("grp", None), spread) + kinds
    out_specs = (spread, spread, spread) + kinds
    return jax.shard_map(body, mesh=mesh, in_specs=in_specs, out_specs=out_specs, check_vma=False)
```

profile of v0, /device:TPU:0, one launch (start us, length us, event | category | flops | bytes accessed | tf_op | source)
XLA Modules:
  0.0 266.1 jit_solution(11151942835893169945)
XLA Ops:
  0.7 111.0 %attention_forward.1 = (bf16[512,768]{1,0:T(8,128)(2,1)}, bf16[3,8,128,128]{3,2,1,0:T(8,128)(2,1)}, bf16[3,8,512,128]{3,2,1,0:T(8,128)(2,1)}, f32[3,8,256,128]{3...) custom-call(s32[1,8]{1,0:T(1,128)} %table.3, ...), custom_call_target="tpu_custom_call" | custom-call | tf_op jit(solution)/shard_map/attention_forward/pallas_call | solution.py:896
  111.7 25.4 %feed_forward.1 = (bf16[512,768]{1,0:T(8,128)(2,1)}, f32[512,768]{1,0:T(8,128)}, bf16[4,3,2,128,128]{4,3,2,1,0:T(8,128)(2,1)}, f32[1,768]{1,0:T(1,128)}, f32[1,7...) custom-call(bf16[12,2,128,128]{3,2,1,0:T(8,128)(2,1)} %get-tuple-ele, ...), custom_call_target="tpu_custom_call" | custom-call | tf_op jit(solution)/shard_map/feed_forward/pallas_call | solution.py:1481
  137.1 124.1 %attention_backward.1 = (f32[512,768]{1,0:T(8,128)}, f32[512,384]{1,0:T(8,128)}, f32[24,3072]{1,0:T(8,128)}, f32[96,768]{1,0:T(8,128)}, f32[24,768]{1,0:T(8,128)...) custom-call(s32[1,8]{1,0:T(1,128)} %table.3, ...), custom_call_target="tpu_custom_call" | custom-call | tf_op jit(solution)/shard_map/attention_backward/pallas_call | solution.py:1297
  261.2 4.7 %hand_over.1 = (f32[512,768]{1,0:T(8,128)}, f32[512,384]{1,0:T(8,128)}, f32[24,768]{1,0:T(8,128)}, f32[24,3072]{1,0:T(8,128)}, f32[96,768]{1,0:T(8,128)}, /*inde...) custom-call(f32[512,768]{1,0:T(8,128)} %get-tuple-element.103.refs_0, ...), custom_call_target="tpu_custom_call" | custom-call | tf_op jit(solution)/shard_map/hand_over/pallas_call | solution.py:1369
where the time goes:
time: 266 us
  Pallas kernels  265 us (100%)
    pallas_call x1, Pallas kernels, backward_call(): pl.pallas_call(functools.partial(backward_kernel, n, groups, heads, [fort...  124 us
    pallas_call x1, Pallas kernels, forward_call(): pl.pallas_call(functools.partial(forward_kernel, n, groups, heads, [forth...  111 us
    pallas_call x1, Pallas kernels, feed_call(): pl.pallas_call(functools.partial(feed_kernel, parts, heads), out_shape=[s...  25.4 us

commit v1 on v0

--- a/solution.py
+++ b/solution.py
@@ -806,7 +806,7 @@
         ol_all[j, place] = jnp.where(lanes(out.shape) < 64, top + jnp.log(denom), out)
 
     later = steps(far, 2)
-    cut = (len(later) // 2, 3 * len(later) // 4)
+    cut = (3 * len(later) // 4, 7 * len(later) // 8)
     for step in later[: cut[0]]:
         step()
     open_vectors(range(4, 9))

time: 266 us -> 265 us (level)
  no operation moved by 1% of the time
where the time goes in v1:
time: 265 us
  Pallas kernels  264 us (100%)
    pallas_call x1, Pallas kernels, backward_call(): pl.pallas_call(functools.partial(backward_kernel, n, groups, heads, [fort...  125 us
    pallas_call x1, Pallas kernels, forward_call(): pl.pallas_call(functools.partial(forward_kernel, n, groups, heads, [forth...  109 us
    pallas_call x1, Pallas kernels, feed_call(): pl.pallas_call(functools.partial(feed_kernel, parts, heads), out_shape=[s...  25.4 us

profile of v1, /device:TPU:0, one launch (start us, length us, event | category | flops | bytes accessed | tf_op | source)
XLA Modules:
  0.0 264.6 jit_solution(14895771744075613723)
XLA Ops:
  0.7 108.9 %attention_forward.1 = (bf16[512,768]{1,0:T(8,128)(2,1)}, bf16[3,8,128,128]{3,2,1,0:T(8,128)(2,1)}, bf16[3,8,512,128]{3,2,1,0:T(8,128)(2,1)}, f32[3,8,256,128]{3...) custom-call(s32[1,8]{1,0:T(1,128)} %table.3, ...), custom_call_target="tpu_custom_call" | custom-call | tf_op jit(solution)/shard_map/attention_forward/pallas_call | solution.py:896
  109.6 25.4 %feed_forward.1 = (bf16[512,768]{1,0:T(8,128)(2,1)}, f32[512,768]{1,0:T(8,128)}, bf16[4,3,2,128,128]{4,3,2,1,0:T(8,128)(2,1)}, f32[1,768]{1,0:T(1,128)}, f32[1,7...) custom-call(bf16[12,2,128,128]{3,2,1,0:T(8,128)(2,1)} %get-tuple-ele, ...), custom_call_target="tpu_custom_call" | custom-call | tf_op jit(solution)/shard_map/feed_forward/pallas_call | solution.py:1481
  135.0 124.7 %attention_backward.1 = (f32[512,768]{1,0:T(8,128)}, f32[512,384]{1,0:T(8,128)}, f32[24,3072]{1,0:T(8,128)}, f32[96,768]{1,0:T(8,128)}, f32[24,768]{1,0:T(8,128)...) custom-call(s32[1,8]{1,0:T(1,128)} %table.3, ...), custom_call_target="tpu_custom_call" | custom-call | tf_op jit(solution)/shard_map/attention_backward/pallas_call | solution.py:1297
  259.7 4.7 %hand_over.1 = (f32[512,768]{1,0:T(8,128)}, f32[512,384]{1,0:T(8,128)}, f32[24,768]{1,0:T(8,128)}, f32[24,3072]{1,0:T(8,128)}, f32[96,768]{1,0:T(8,128)}, /*inde...) custom-call(f32[512,768]{1,0:T(8,128)} %get-tuple-element.103.refs_0, ...), custom_call_target="tpu_custom_call" | custom-call | tf_op jit(solution)/shard_map/hand_over/pallas_call | solution.py:1369

commit v2 on v1

--- a/solution.py
+++ b/solution.py
@@ -598,7 +598,7 @@
 
     def scatter(self, j, staged, landed, send, recv):
         out = []
-        for off in range(1, self.n):
+        for off in sorted(range(1, self.n), key=lambda o: abs(o - self.n // 2)):
             t = self.other(off)
             out.append(remote(staged.at[t // self.splits, j, lax.rem(t, self.splits)], landed.at[j, self.s],
                               send.at[j, off - 1], recv.at[j, self.s], {"seq": t}))
@@ -609,7 +609,7 @@
 
     def spread(self, j, staged, landed, send, recv):
         out = []
-        for off in range(1, PARTS):
+        for off in sorted(range(1, PARTS), key=lambda o: abs(o - PARTS // 2)):
             part = lax.rem(self.part + off, PARTS)
             out.append(remote(staged.at[part, j], landed.at[j, self.s], send.at[j, off - 1],
                               recv.at[j, self.s], {"seq": part * self.splits + self.split}))
@@ -630,7 +630,7 @@
     def give_back(self, j, heads, staged, landed, send, recv):
         out = []
         row = self.part * heads + j
-        for off in range(1, self.n):
+        for off in sorted(range(1, self.n), key=lambda o: abs(o - self.n // 2)):
             t = self.other(off)
             out.append(remote(staged.at[j, t], landed.at[row, self.split], send.at[j, off - 1],
                               recv.at[j, self.s], {"seq": t}))

time: 265 us -> 264 us (level)
  no operation moved by 1% of the time
where the time goes in v2:
time: 264 us
  Pallas kernels  263 us (100%)
    pallas_call x1, Pallas kernels, backward_call(): pl.pallas_call(functools.partial(backward_kernel, n, groups, heads, [fort...  124 us
    pallas_call x1, Pallas kernels, forward_call(): pl.pallas_call(functools.partial(forward_kernel, n, groups, heads, [forth...  109 us
    pallas_call x1, Pallas kernels, feed_call(): pl.pallas_call(functools.partial(feed_kernel, parts, heads), out_shape=[s...  25.4 us

profile of v2, /device:TPU:0, one launch (start us, length us, event | category | flops | bytes accessed | tf_op | source)
XLA Modules:
  0.0 263.9 jit_solution(114092460110433786)
XLA Ops:
  0.7 109.4 %attention_forward.1 = (bf16[512,768]{1,0:T(8,128)(2,1)}, bf16[3,8,128,128]{3,2,1,0:T(8,128)(2,1)}, bf16[3,8,512,128]{3,2,1,0:T(8,128)(2,1)}, f32[3,8,256,128]{3...) custom-call(s32[1,8]{1,0:T(1,128)} %table.3, ...), custom_call_target="tpu_custom_call" | custom-call | tf_op jit(solution)/shard_map/attention_forward/pallas_call | solution.py:896
  110.0 25.4 %feed_forward.1 = (bf16[512,768]{1,0:T(8,128)(2,1)}, f32[512,768]{1,0:T(8,128)}, bf16[4,3,2,128,128]{4,3,2,1,0:T(8,128)(2,1)}, f32[1,768]{1,0:T(1,128)}, f32[1,7...) custom-call(bf16[12,2,128,128]{3,2,1,0:T(8,128)(2,1)} %get-tuple-ele, ...), custom_call_target="tpu_custom_call" | custom-call | tf_op jit(solution)/shard_map/feed_forward/pallas_call | solution.py:1481
  135.5 123.5 %attention_backward.1 = (f32[512,768]{1,0:T(8,128)}, f32[512,384]{1,0:T(8,128)}, f32[24,3072]{1,0:T(8,128)}, f32[96,768]{1,0:T(8,128)}, f32[24,768]{1,0:T(8,128)...) custom-call(s32[1,8]{1,0:T(1,128)} %table.3, ...), custom_call_target="tpu_custom_call" | custom-call | tf_op jit(solution)/shard_map/attention_backward/pallas_call | solution.py:1297
  259.0 4.7 %hand_over.1 = (f32[512,768]{1,0:T(8,128)}, f32[512,384]{1,0:T(8,128)}, f32[24,768]{1,0:T(8,128)}, f32[24,3072]{1,0:T(8,128)}, f32[96,768]{1,0:T(8,128)}, /*inde...) custom-call(f32[512,768]{1,0:T(8,128)} %get-tuple-element.103.refs_0, ...), custom_call_target="tpu_custom_call" | custom-call | tf_op jit(solution)/shard_map/hand_over/pallas_call | solution.py:1369
